TPU v7x, 32 devices: a whole 2x2x4 slice. The times are simulated.
32 devices in a mesh: grp: 4 (over z), mem: 8 (over y, x, core).
Axes of the slice: x: 2, y: 2, z: 4, core: 2. Of those that a mesh axis runs over, the one named last changes fastest.
Arguments:
- child_means: float32 [65536, 64], P(('grp', 'mem')), may hold values from -48 to 48
- child_variances: float32 [65536, 64], P(('grp', 'mem')), may hold values from 0.2 to 2
- virtual_counts: int32 [65536], P(('grp', 'mem')), may hold values from 1 to 4
- assignment: int32 [65536, 1], P(('grp', 'mem')), may hold values from 0 to 511
Outputs:
- parent_means: float32 [512, 64], P('mem')
- parent_variances: float32 [512, 64], P('mem')
- parent_weights: float32 [512], P('mem')
All inputs are finite; a program needn't handle non-finite values.
Results may differ from a plain program's by a relative error of at most 0.0003.
Values sent between devices are 32-bit elements; how exact they have to be, the bound alone decides.
A program may use at most 64 MiB of HBM per device.

v0:
```python
import math
import jax
import jax.numpy as jnp
from jax import lax
from jax.sharding import PartitionSpec as P

P_SIZE = 512
ITERS = 2


def child_features(means, variances):
    return jnp.concatenate([means, variances + means * means], axis=1)


def accumulate(features, extras, weigh):
    row_count = features.shape[0]
    block = math.gcd(row_count, 1024)
    turns = row_count // block
    pieces = (features.reshape(turns, block, features.shape[1]),) + tuple(
        (extra.reshape((turns, block) + extra.shape[1:]) for extra in extras)
    )

    def advance(carry, piece):
        weights = weigh(*piece)
        sums = carry[0] + lax.dot_general(
            weights,
            piece[0],
            (((0,), (0,)), ((), ())),
            precision=lax.Precision.HIGHEST,
            preferred_element_type=jnp.float32,
        )
        counts = carry[1] + jnp.sum(weights, axis=0)
        return ((sums, counts), None)

    start_sums = (
        jnp.zeros((P_SIZE, features.shape[1]), jnp.float32),
        jnp.zeros((P_SIZE,), jnp.float32),
    )
    return lax.scan(advance, start_sums, pieces)[0]


def maximize(counts, sums, total):
    width = sums.shape[1] // 2
    mass = counts + 1.0
    means = sums[:, :width] / mass[:, None]
    second = (sums[:, width:] + 1.0) / mass[:, None]
    return (means, second - means * means, mass / (total + P_SIZE))


def parent_table(means, variances, weights):
    inverse = 1.0 / variances
    table = jnp.concatenate([-2.0 * means * inverse, inverse], axis=1)
    offset = jnp.sum(jnp.log(2.0 * math.pi * variances) + means * means * inverse, axis=1)
    return (table, offset, jnp.log(weights))


def soft_weights(block_features, block_virtual, table, offset, log_weight):
    width = block_features.shape[1] // 2
    cross = lax.dot_general(
        block_features,
        table,
        (((1,), (1,)), ((), ())),
        precision=lax.Precision.HIGHEST,
        preferred_element_type=jnp.float32,
    )
    ell = -0.5 / width * (cross + offset[None, :])
    score = log_weight[None, :] + block_virtual[:, None] * ell
    top = jnp.max(score, axis=1, keepdims=True)
    expd = jnp.exp(score - top)
    resp = expd / jnp.sum(expd, axis=1, keepdims=True)
    return resp * block_virtual[:, None]


def shards(child_means, child_variances, virtual_counts, assignment):
    features = child_features(child_means, child_variances)
    virtual = virtual_counts.astype(jnp.float32)
    labels = jnp.arange(P_SIZE, dtype=jnp.int32)

    def initial_weights(block_features, block_virtual, block_assign):
        return (block_assign == labels[None, :]).astype(jnp.float32) * block_virtual[:, None]

    sums, counts = accumulate(features, (virtual, assignment), initial_weights)
    total = lax.psum(jnp.sum(virtual), ("grp", "mem"))

    def combine(local_sums, local_counts):
        shared = (
            lax.psum_scatter(local_sums, "mem", scatter_dimension=0, tiled=True),
            lax.psum_scatter(local_counts, "mem", scatter_dimension=0, tiled=True),
        )
        return lax.psum((shared[0], shared[1]), "grp")

    own_sums, own_counts = combine(sums, counts)
    means, variances, weights = maximize(own_counts, own_sums, total)
    for iteration in range(ITERS):
        all_means, all_variances, all_weights = (
            lax.all_gather(means, "mem", axis=0, tiled=True),
            lax.all_gather(variances, "mem", axis=0, tiled=True),
            lax.all_gather(weights, "mem", axis=0, tiled=True),
        )
        table, offset, log_weight = parent_table(all_means, all_variances, all_weights)

        def weigh(block_features, block_virtual):
            return soft_weights(block_features, block_virtual, table, offset, log_weight)

        sums, counts = accumulate(features, (virtual,), weigh)
        own_sums, own_counts = combine(sums, counts)
        means, variances, weights = maximize(own_counts, own_sums, total)
    return (means, variances, weights)


def solution(mesh):
    in_specs = (
        P(("grp", "mem"), None),
        P(("grp", "mem"), None),
        P(("grp", "mem")),
        P(("grp", "mem"), None),
    )
    out_specs = (P("mem", None), P("mem", None), P("mem"))
    return jax.shard_map(shards, mesh=mesh, in_specs=in_specs, out_specs=out_specs, check_vma=False)
```

profile of v0, /device:TPU:0, one launch (start us, length us, event | category | flops | bytes accessed | tf_op | source)
XLA Modules:
  0.0 293.5 jit_solution(11252077472539837460)
XLA Ops:
  7.2 1.3 multiply_add_fusion.2
  8.5 1.2 pad_maximum_fusion
  9.7 0.3 copy.9
  10.1 8.4 %while.39 = (s32[]{:T(128)}, f32[512,128]{1,0:T(8,128)S(1)}, f32[512]{0:T(512)S(1)}, s32[2,1024,1]{1,2,0:T(1,128)S(1)}, f32[2,1024]{1,0:T(2,128)S(1)}, /*index=5*/f32[2,1024,128]{2,1,0:T(8,128)S(1)}, s32[]{:T(128)}, s32[]{:T(128)}) while((s32[]{:T(128)}, f32[512,128]{1,0:T(8,128)S(1)}, f32[512]{0:T(512)S(1)}, ...), condition=%wide.region_2.3_spmd.clone, body=%wide.region_0.2_spmd.clone.sunk | while | flops 808059392 | bytes 1089644 | solution.py:39
  10.1 3.8 %fusion.56 = f32[512,128]{1,0:T(8,128)S(1)} fusion(f32[1024]{0:T(1024)S(1)} %bitcast.56, s32[1024]{0:T(1024)S(1)} %bitcast.58, f32[2,1024,128]{2,1,0:T(8,128)S(1)} %get-tuple-element.448, s32[]{:T(128)} %get-tuple-element.435, f32[512,128]{1,0:T(8,128)S(1)} %get-tuple-element.436, pred[]{:T(512)S(6)} %compare.9), kind=kOutput, calls=%fused_computation.5.clone.1 | convolution fusion | flops 806486016 | bytes 1056773 | tf_op jit(solution)/shard_map/while/body/eval_jaxpr/dot_general | solution.py:25
  13.9 0.3 select_reduce_fusion.2
  14.3 3.8 %fusion.56 = f32[512,128]{1,0:T(8,128)S(1)} fusion(f32[1024]{0:T(1024)S(1)} %bitcast.56, s32[1024]{0:T(1024)S(1)} %bitcast.58, f32[2,1024,128]{2,1,0:T(8,128)S(1)} %get-tuple-element.448, s32[]{:T(128)} %get-tuple-element.435, f32[512,128]{1,0:T(8,128)S(1)} %get-tuple-element.436, pred[]{:T(512)S(6)} %compare.9), kind=kOutput, calls=%fused_computation.5.clone.1 | convolution fusion | flops 806486016 | bytes 1056773 | tf_op jit(solution)/shard_map/while/body/eval_jaxpr/dot_general | solution.py:25
  18.1 0.3 select_reduce_fusion.2
  18.5 0.7 copy-done
  19.2 0.6 convert_reduce_fusion
  19.8 42.2 %psum.50 = f32[]{:T(128)} all-reduce(f32[]{:T(128)} %convert_reduce_fusion), channel_id=1, replica_groups=mesh['grp'=4,'mem'=8] {'grp','mem'}, use_global_device_ids=true, to_apply=%region_9.10 | all-reduce | flops 1 | bytes 8 | tf_op jit(solution)/shard_map/psum | solution.py:83
  62.0 0.6 fusion.38
  63.2 13.0 %all-reduce.2 = f32[512]{0:T(512)S(1)} all-reduce(f32[512]{0:T(512)S(1)} %get-tuple-element.127), channel_id=2, replica_groups=mesh['grp'=4,'mem'=8] {'mem'}, use_global_device_ids=true, to_apply=%region_5.6.clone | all-reduce | flops 512 | bytes 4096
  77.6 18.8 %all-reduce.7 = (f32[64]{0:T(128)S(1)}, f32[64,128]{1,0:T(8,128)S(1)}) all-reduce(f32[64]{0:T(128)S(1)} %dynamic-slice.3, f32[64,128]{1,0:T(8,128)} %reduce-scatter.4.cloned.1.call-done), channel_id=1, replica_groups=mesh['grp'=4,'mem'=8] {'grp'}, use_global_device_ids=true, to_apply=%region_6.7 | all-reduce | flops 8256 | bytes 66048 | tf_op jit(solution)/shard_map/psum | solution.py:90
  96.6 9.1 %all_gather.19 = f32[512,64]{1,0:T(8,128)S(1)} all-gather(f32[64,64]{1,0:T(8,128)S(1)} %get-tuple-element.274), channel_id=1, replica_groups=mesh['grp'=4,'mem'=8] {'mem'}, dimensions={0}, use_global_device_ids=true | all-gather | bytes 147456 | tf_op jit(solution)/shard_map/all_gather | solution.py:96
  105.7 8.5 %all_gather.20 = f32[512,64]{1,0:T(8,128)S(1)} all-gather(f32[64,64]{1,0:T(8,128)S(1)} %get-tuple-element.275), channel_id=1, replica_groups=mesh['grp'=4,'mem'=8] {'mem'}, dimensions={0}, use_global_device_ids=true | all-gather | bytes 147456 | tf_op jit(solution)/shard_map/all_gather | solution.py:97
  114.2 13.4 %all-reduce = f32[512]{0:T(512)S(1)} all-reduce(f32[512]{0:T(512)S(1)} %get-tuple-element.281), channel_id=1, replica_groups=mesh['grp'=4,'mem'=8] {'mem'}, use_global_device_ids=true, to_apply=%add | all-reduce | flops 512 | bytes 4096
  127.6 0.2 add_reduce_fusion.1
  127.9 12.2 %while.40 = (s32[]{:T(128)}, f32[512,128]{1,0:T(8,128)}, f32[512]{0:T(512)S(1)}, f32[512]{0:T(512)S(1)}, f32[2,1024,128]{2,1,0:T(8,128)S(1)}, /*index=5*/f32[512...) while((s32[]{:T(128)}, f32[512,128]{1,0:T(8,128)}, ...), condition=%wide.region_14.15_spmd.clone, body=%wide.region_10.14_spmd.clone.sunk | while | flops 1617559040 | bytes 10293372 | solution.py:39
  127.9 2.0 fusion.59
  130.0 0.3 fusion.60
  130.3 0.5 fusion.61
  130.8 2.7 convolution_add_fusion.4
  133.6 2.0 fusion.59
  135.6 0.3 fusion.60
  135.9 0.5 fusion.61
  136.5 3.7 %convolution_add_fusion.4 = f32[512,128]{1,0:T(8,128)} fusion(f32[2,1024,128]{2,1,0:T(8,128)S(1)} %get-tuple-element.475, s32[]{:T(128)} %get-tuple-element.461, f32[1024,512]{0,1:T(8,128)S(1)} %get-tuple-element.415, f32[1024]{0:T(1024)S(1)} %bitcast.52, f32[1024]{0:T(1024)S(1)} %fusion.60, f32[1024]{0:T(1024)S(1)} %get-tuple-element.416, ...), kind=kOutput, calls=%fused_computation.20.clone.1 | convolution fusion | flops 807010304 | bytes 3158021 | tf_op jit(solution)/shard_map/while/body/eval_jaxpr/dot_general | solution.py:25
  140.2 11.8 %all-reduce.3 = f32[512]{0:T(512)S(1)} all-reduce(f32[512]{0:T(512)S(1)} %get-tuple-element.129), channel_id=4, replica_groups=mesh['grp'=4,'mem'=8] {'mem'}, use_global_device_ids=true, to_apply=%region_17.18.clone | all-reduce | flops 512 | bytes 4096
  152.1 19.0 %reduce-scatter.6.cloned.1.call-done = f32[64,128]{1,0:T(8,128)} async-done(((f32[512,128]{1,0:T(8,128)}), f32[64,128]{1,0:T(8,128)}) %reduce-scatter.6.cloned.1.call-update) | async-done | bytes 32784 | tf_op jit(solution)/shard_map/reduce_scatter | solution.py:87
  171.1 19.9 %all-reduce.6 = (f32[64]{0:T(128)S(1)}, f32[64,128]{1,0:T(8,128)S(1)}) all-reduce(f32[64]{0:T(128)S(1)} %dynamic-slice.5, f32[64,128]{1,0:T(8,128)} %reduce-scatter.6.cloned.1.call-done), channel_id=1, replica_groups=mesh['grp'=4,'mem'=8] {'grp'}, use_global_device_ids=true, to_apply=%region_18.19 | all-reduce | flops 8256 | bytes 66048 | tf_op jit(solution)/shard_map/psum | solution.py:90
  191.2 9.3 %all_gather.22 = f32[512,64]{1,0:T(8,128)S(1)} all-gather(f32[64,64]{1,0:T(8,128)S(1)} %get-tuple-element.272), channel_id=1, replica_groups=mesh['grp'=4,'mem'=8] {'mem'}, dimensions={0}, use_global_device_ids=true | all-gather | bytes 147456 | tf_op jit(solution)/shard_map/all_gather | solution.py:96
  200.4 8.3 %all_gather.23 = f32[512,64]{1,0:T(8,128)S(1)} all-gather(f32[64,64]{1,0:T(8,128)S(1)} %get-tuple-element.273), channel_id=1, replica_groups=mesh['grp'=4,'mem'=8] {'mem'}, dimensions={0}, use_global_device_ids=true | all-gather | bytes 147456 | tf_op jit(solution)/shard_map/all_gather | solution.py:97
  208.8 13.4 %all-reduce.1 = f32[512]{0:T(512)S(1)} all-reduce(f32[512]{0:T(512)S(1)} %get-tuple-element.279), channel_id=1, replica_groups=mesh['grp'=4,'mem'=8] {'mem'}, use_global_device_ids=true, to_apply=%add.1 | all-reduce | flops 512 | bytes 4096
  222.2 0.2 add_reduce_fusion
  222.5 12.2 %while.41 = (s32[]{:T(128)}, f32[512,128]{1,0:T(8,128)}, f32[512]{0:T(512)S(1)}, f32[512]{0:T(512)S(1)}, f32[2,1024,128]{2,1,0:T(8,128)S(1)}, /*index=5*/f32[512...) while((s32[]{:T(128)}, f32[512,128]{1,0:T(8,128)}, ...), condition=%wide.region_24.25_spmd.clone, body=%wide.region_20.24_spmd.clone.sunk | while | flops 1617559040 | bytes 10293372 | solution.py:39
  222.5 2.0 fusion.64
  224.6 0.3 fusion.65
  224.9 0.5 fusion.66
  225.4 2.7 convolution_add_fusion.5
  228.2 2.0 fusion.64
  230.2 0.3 fusion.65
  230.5 0.5 fusion.66
  231.1 3.7 %convolution_add_fusion.5 = f32[512,128]{1,0:T(8,128)} fusion(f32[2,1024,128]{2,1,0:T(8,128)S(1)} %get-tuple-element.505, s32[]{:T(128)} %get-tuple-element.491, f32[1024,512]{0,1:T(8,128)S(1)} %get-tuple-element.425, f32[1024]{0:T(1024)S(1)} %bitcast.55, f32[1024]{0:T(1024)S(1)} %fusion.65, f32[1024]{0:T(1024)S(1)} %get-tuple-element.426, ...), kind=kOutput, calls=%fused_computation.35.clone.1 | convolution fusion | flops 807010304 | bytes 3158021 | tf_op jit(solution)/shard_map/while/body/eval_jaxpr/dot_general | solution.py:25
  234.7 11.8 %all-reduce.4 = f32[512]{0:T(512)S(1)} all-reduce(f32[512]{0:T(512)S(1)} %get-tuple-element.132), channel_id=7, replica_groups=mesh['grp'=4,'mem'=8] {'mem'}, use_global_device_ids=true, to_apply=%region_27.28.clone | all-reduce | flops 512 | bytes 4096
  246.6 19.2 %reduce-scatter.8.cloned.1.call-done = f32[64,128]{1,0:T(8,128)} async-done(((f32[512,128]{1,0:T(8,128)}), f32[64,128]{1,0:T(8,128)}) %reduce-scatter.8.cloned.1.call-update) | async-done | bytes 32784 | tf_op jit(solution)/shard_map/reduce_scatter | solution.py:87
  265.8 19.9 %all-reduce.5 = (f32[64,128]{1,0:T(8,128)S(1)}, f32[64]{0:T(128)S(1)}) all-reduce(f32[64,128]{1,0:T(8,128)} %reduce-scatter.8.cloned.1.call-done, f32[64]{0:T(128)S(1)} %dynamic-slice.7), channel_id=1, replica_groups=mesh['grp'=4,'mem'=8] {'grp'}, use_global_device_ids=true, to_apply=%region_26.27 | all-reduce | flops 8256 | bytes 66048 | tf_op jit(solution)/shard_map/psum | solution.py:90
  285.7 0.5 broadcast_divide_fusion.2
  286.2 0.7 fusion.31
  (53 shorter events, 1.3 us)
Async XLA Ops:
  7.2 70.4 %reduce-scatter.4.cloned.1.call-start = ((), (), s32[]{:S(2)}) async-start(), calls=%async_computation.3 | async-start | bytes 294912 | tf_op jit(solution)/shard_map/reduce_scatter | solution.py:87
  8.5 1.5 copy-start.2
  8.5 1.5 copy-start.1
  10.1 51.9 %copy-start.3 = (u32[32]{0:T(128)S(1)}, u32[32]{0:T(128)}, u32[]{:S(2)}) copy-start(u32[32]{0:T(128)} %constant.58) | copy-start | bytes 388
  18.5 0.7 copy-start
  19.2 151.9 %reduce-scatter.6.cloned.1.call-start = ((), (), s32[]{:S(2)}) async-start(), calls=%async_computation.4 | async-start | bytes 294912 | tf_op jit(solution)/shard_map/reduce_scatter | solution.py:87
  140.1 125.7 %reduce-scatter.8.cloned.1.call-start = ((), (), s32[]{:S(2)}) async-start(), calls=%async_computation.5 | async-start | bytes 294912 | tf_op jit(solution)/shard_map/reduce_scatter | solution.py:87
Sparse Core Ops, SparseCore 0:
  19.3 36.3 reduce-scatter.3
  140.3 30.7 reduce-scatter.5
  234.9 30.9 reduce-scatter.7
where the time goes:
time: 294 us; the launch traced here: 293 us
  blocking collectives  199 us (68%)
  waiting for transfers between devices  38.3 us (13%)
  matrix products  28.4 us (10%)
  between operations  15.9 us (5%)
  other arithmetic  9.37 us (3%)
    unnamed x5, blocking collectives  63.3 us
    psum x3, blocking collectives, combine(): return lax.psum((shared[0], shared[1]), 'grp')  58.5 us
    psum x1, blocking collectives, shards(): total = lax.psum(jnp.sum(virtual), ('grp', 'mem'))  42.2 us
    reduce_scatter x3, waiting for transfers between devices, combine(): lax.psum_scatter(local_sums, 'mem', scatter_dimension=0, tiled=True)  38.2 us
    dot_general x6, matrix products, advance(): lax.dot_general(weights, piece[0], (((0,), (0,)), ((), ())), precision=la...  20.3 us
    all_gather x2, blocking collectives, shards(): lax.all_gather(means, 'mem', axis=0, tiled=True)  18.4 us
    all_gather x2, blocking collectives, shards(): lax.all_gather(variances, 'mem', axis=0, tiled=True)  16.8 us
    dot_general x4, matrix products, soft_weights(): lax.dot_general(block_features, table, (((1,), (1,)), ((), ())), precisio...  8.14 us
  transfers between devices with their start and end apart: 3, of which 2 were waited for; matrix products, arithmetic and copies ran while one was open for 0% of the time, Pallas kernels for 0%

commit v1 on v0

--- a/solution.py
+++ b/solution.py
@@ -1,3 +1,4 @@
+import functools
 import math
 import jax
 import jax.numpy as jnp
@@ -6,6 +7,36 @@
 
 P_SIZE = 512
 ITERS = 2
+
+
+def spot_list(xin, where_dim):
+    xin = jnp.moveaxis(xin, 0, where_dim)
+    reply = xin.shape
+    found_now = xin.reshape(
+        *reply[:where_dim], reply[where_dim] * reply[where_dim + 1], *reply[where_dim + 2 :]
+    )
+    return found_now
+
+
+def lots_all_keep_up(chunk, across):
+    chips = lax.psum(1, across)
+    arr_out = chunk[None]
+    for at in range(chips.bit_length() - 1):
+        even = 1 << at
+        frame_out = lax.ppermute(arr_out, across, [(jj, jj ^ even) for jj in range(chips)])
+        response = jnp.stack([arr_out, frame_out], axis=0)
+        aux = lax.axis_index(across) >> at & 1
+        arr_out = jnp.where(aux == 0, response, response[::-1]).reshape(-1, *chunk.shape)
+    return arr_out
+
+
+def tracks_tell(mat, buf, dim_at):
+    y = lots_all_keep_up(mat, buf)
+    o_now = spot_list(y, dim_at)
+    return o_now
+
+
+supply_the_positions = functools.partial(tracks_tell, buf="mem", dim_at=0)
 
 
 def child_features(means, variances):
@@ -94,7 +125,7 @@
     for iteration in range(ITERS):
         all_means, all_variances, all_weights = (
             lax.all_gather(means, "mem", axis=0, tiled=True),
-            lax.all_gather(variances, "mem", axis=0, tiled=True),
+            supply_the_positions(variances),
             lax.all_gather(weights, "mem", axis=0, tiled=True),
         )
         table, offset, log_weight = parent_table(all_means, all_variances, all_weights)

time: 294 us -> 288 us (0.980)
  blocking collectives: 199 us -> 181 us
  waiting for transfers between devices: 38.3 us -> 45.1 us
  starting transfers between devices: 0.12 us -> 4.85 us
    all_gather x2 -> x0, blocking collectives: 16.8 us -> none  [shards(): lax.all_gather(variances, 'mem', axis=0, tiled=True)]
    ppermute x0 -> x6, waiting for transfers between devices: none -> 9.43 us  [lots_all_keep_up(): lax.ppermute(arr_out, across, [(jj, jj ^ even) for jj in range(chips)])]
    ppermute x0 -> x6, starting transfers between devices: none -> 4.73 us  [lots_all_keep_up(): lax.ppermute(arr_out, across, [(jj, jj ^ even) for jj in range(chips)])]
  transfers between devices with their start and end apart: 3 -> 9, of which waited for: 2 -> 6; matrix products, arithmetic and copies ran while one was open for 0% -> 1% of each run, Pallas kernels for 0% -> 0%
where the time goes in v1:
time: 288 us; the launch traced here: 287 us
  blocking collectives  181 us (63%)
  waiting for transfers between devices  45.1 us (16%)
  matrix products  28.4 us (10%)
  between operations  16 us (6%)
  other arithmetic  9.61 us (3%)
  starting transfers between devices  4.85 us (2%)
    unnamed x5, blocking collectives  62.9 us
    psum x3, blocking collectives, combine(): return lax.psum((shared[0], shared[1]), 'grp')  58.4 us
    psum x1, blocking collectives, shards(): total = lax.psum(jnp.sum(virtual), ('grp', 'mem'))  42.2 us
    reduce_scatter x3, waiting for transfers between devices, combine(): lax.psum_scatter(local_sums, 'mem', scatter_dimension=0, tiled=True)  35.6 us
    dot_general x6, matrix products, advance(): lax.dot_general(weights, piece[0], (((0,), (0,)), ((), ())), precision=la...  20.3 us
    all_gather x2, blocking collectives, shards(): lax.all_gather(means, 'mem', axis=0, tiled=True)  17.2 us
    ppermute x6, waiting for transfers between devices, lots_all_keep_up(): lax.ppermute(arr_out, across, [(jj, jj ^ even) for jj in range(chips)])  9.43 us
    dot_general x4, matrix products, soft_weights(): lax.dot_general(block_features, table, (((1,), (1,)), ((), ())), precisio...  8.15 us
  transfers between devices with their start and end apart: 9, of which 6 were waited for; matrix products, arithmetic and copies ran while one was open for 1% of the time, Pallas kernels for 0%

profile of v1, /device:TPU:0, one launch (start us, length us, event | category | flops | bytes accessed | tf_op | source)
XLA Modules:
  0.0 286.9 jit_solution(17092758935250527949)
XLA Ops:
  7.2 1.3 multiply_add_fusion.2
  8.5 1.2 pad_maximum_fusion
  10.1 8.4 %while.39 = (s32[]{:T(128)}, f32[512,128]{1,0:T(8,128)S(1)}, f32[512]{0:T(512)S(1)}, s32[2,1024,1]{1,2,0:T(1,128)S(1)}, f32[2,1024]{1,0:T(2,128)S(1)}, /*index=5*/f32[2,1024,128]{2,1,0:T(8,128)S(1)}, s32[]{:T(128)}, s32[]{:T(128)}) while((s32[]{:T(128)}, f32[512,128]{1,0:T(8,128)S(1)}, f32[512]{0:T(512)S(1)}, ...), condition=%wide.region_2.3_spmd.clone, body=%wide.region_0.2_spmd.clone.sunk | while | flops 808059392 | bytes 1089644 | solution.py:70
  10.1 3.8 %fusion.68 = f32[512,128]{1,0:T(8,128)S(1)} fusion(f32[1024]{0:T(1024)S(1)} %bitcast.110, s32[1024]{0:T(1024)S(1)} %bitcast.112, f32[2,1024,128]{2,1,0:T(8,128)S(1)} %get-tuple-element.456, s32[]{:T(128)} %get-tuple-element.443, f32[512,128]{1,0:T(8,128)S(1)} %get-tuple-element.444, pred[]{:T(512)S(6)} %compare.9), kind=kOutput, calls=%fused_computation.5.clone.1 | convolution fusion | flops 806486016 | bytes 1056773 | tf_op jit(solution)/shard_map/while/body/eval_jaxpr/dot_general | solution.py:56
  13.9 0.3 select_reduce_fusion.2
  14.3 3.8 %fusion.68 = f32[512,128]{1,0:T(8,128)S(1)} fusion(f32[1024]{0:T(1024)S(1)} %bitcast.110, s32[1024]{0:T(1024)S(1)} %bitcast.112, f32[2,1024,128]{2,1,0:T(8,128)S(1)} %get-tuple-element.456, s32[]{:T(128)} %get-tuple-element.443, f32[512,128]{1,0:T(8,128)S(1)} %get-tuple-element.444, pred[]{:T(512)S(6)} %compare.9), kind=kOutput, calls=%fused_computation.5.clone.1 | convolution fusion | flops 806486016 | bytes 1056773 | tf_op jit(solution)/shard_map/while/body/eval_jaxpr/dot_general | solution.py:56
  18.1 0.3 select_reduce_fusion.2
  18.5 0.7 copy-done
  19.2 0.6 convert_reduce_fusion
  19.8 42.2 %psum.50 = f32[]{:T(128)} all-reduce(f32[]{:T(128)} %convert_reduce_fusion), channel_id=1, replica_groups=mesh['grp'=4,'mem'=8] {'grp','mem'}, use_global_device_ids=true, to_apply=%region_9.10 | all-reduce | flops 1 | bytes 8 | tf_op jit(solution)/shard_map/psum | solution.py:114
  62.0 0.6 fusion.50
  63.2 12.9 %all-reduce.2 = f32[512]{0:T(512)S(1)} all-reduce(f32[512]{0:T(512)S(1)} %get-tuple-element.127), channel_id=2, replica_groups=mesh['grp'=4,'mem'=8] {'mem'}, use_global_device_ids=true, to_apply=%region_5.6.clone | all-reduce | flops 512 | bytes 4096
  77.5 18.7 %all-reduce.7 = (f32[64]{0:T(128)S(1)}, f32[64,128]{1,0:T(8,128)S(1)}) all-reduce(f32[64]{0:T(128)S(1)} %dynamic-slice.3, f32[64,128]{1,0:T(8,128)} %reduce-scatter.4.cloned.1.call-done), channel_id=1, replica_groups=mesh['grp'=4,'mem'=8] {'grp'}, use_global_device_ids=true, to_apply=%region_6.7 | all-reduce | flops 8256 | bytes 66048 | tf_op jit(solution)/shard_map/psum | solution.py:121
  96.6 1.2 collective-permute-done
  97.9 4.2 %collective-permute-done.1 = f32[2,64,64]{2,1,0:T(8,128)S(1)} collective-permute-done((f32[2,64,64]{2,1,0:T(8,128)S(1)}, f32[2,64,64]{2,1,0:T(8,128)S(1)}, u32[]{:S(2)}, u32[]{:S(2)}) %collective-permute-start.1) | collective-permute-done | bytes 32800 | tf_op jit(solution)/shard_map/ppermute | solution.py:26
  102.1 1.5 collective-permute-start.2
  103.6 11.8 %all-reduce = f32[512]{0:T(512)S(1)} all-reduce(f32[512]{0:T(512)S(1)} %get-tuple-element.289), channel_id=1, replica_groups=mesh['grp'=4,'mem'=8] {'mem'}, use_global_device_ids=true, to_apply=%add | all-reduce | flops 512 | bytes 4096
  115.4 8.6 %all_gather.13 = f32[512,64]{1,0:T(8,128)S(1)} all-gather(f32[64,64]{1,0:T(8,128)S(1)} %get-tuple-element.281), channel_id=1, replica_groups=mesh['grp'=4,'mem'=8] {'mem'}, dimensions={0}, use_global_device_ids=true | all-gather | bytes 147456 | tf_op jit(solution)/shard_map/all_gather | solution.py:127
  124.4 12.2 %while.40 = (s32[]{:T(128)}, f32[512,128]{1,0:T(8,128)}, f32[512]{0:T(512)S(1)}, f32[512]{0:T(512)S(1)}, f32[2,1024,128]{2,1,0:T(8,128)S(1)}, /*index=5*/f32[512...) while((s32[]{:T(128)}, f32[512,128]{1,0:T(8,128)}, ...), condition=%wide.region_14.15_spmd.clone, body=%wide.region_10.14_spmd.clone.sunk | while | flops 1617559040 | bytes 10293372 | solution.py:70
  124.4 2.0 fusion.71
  126.5 0.3 fusion.72
  126.8 0.5 fusion.73
  127.3 2.7 convolution_add_fusion.4
  130.1 2.0 fusion.71
  132.1 0.3 fusion.72
  132.5 0.5 fusion.73
  133.0 3.7 %convolution_add_fusion.4 = f32[512,128]{1,0:T(8,128)} fusion(f32[2,1024,128]{2,1,0:T(8,128)S(1)} %get-tuple-element.483, s32[]{:T(128)} %get-tuple-element.469, f32[1024,512]{0,1:T(8,128)S(1)} %get-tuple-element.423, f32[1024]{0:T(1024)S(1)} %bitcast.102, f32[1024]{0:T(1024)S(1)} %fusion.72, f32[1024]{0:T(1024)S(1)} %get-tuple-element.424, ...), kind=kOutput, calls=%fused_computation.20.clone.1 | convolution fusion | flops 807010304 | bytes 3158021 | tf_op jit(solution)/shard_map/while/body/eval_jaxpr/dot_general | solution.py:56
  136.7 13.2 %all-reduce.3 = f32[512]{0:T(512)S(1)} all-reduce(f32[512]{0:T(512)S(1)} %get-tuple-element.129), channel_id=4, replica_groups=mesh['grp'=4,'mem'=8] {'mem'}, use_global_device_ids=true, to_apply=%region_17.18.clone | all-reduce | flops 512 | bytes 4096
  150.0 17.8 %reduce-scatter.6.cloned.1.call-done = f32[64,128]{1,0:T(8,128)} async-done(((f32[512,128]{1,0:T(8,128)}), f32[64,128]{1,0:T(8,128)}) %reduce-scatter.6.cloned.1.call-update) | async-done | bytes 32784 | tf_op jit(solution)/shard_map/reduce_scatter | solution.py:118
  167.8 19.9 %all-reduce.6 = (f32[64]{0:T(128)S(1)}, f32[64,128]{1,0:T(8,128)S(1)}) all-reduce(f32[64]{0:T(128)S(1)} %dynamic-slice.5, f32[64,128]{1,0:T(8,128)} %reduce-scatter.6.cloned.1.call-done), channel_id=1, replica_groups=mesh['grp'=4,'mem'=8] {'grp'}, use_global_device_ids=true, to_apply=%region_18.19 | all-reduce | flops 8256 | bytes 66048 | tf_op jit(solution)/shard_map/psum | solution.py:121
  187.9 1.2 collective-permute-done.3
  189.1 1.5 collective-permute-start.4
  190.7 2.8 collective-permute-done.4
  193.5 1.5 collective-permute-start.5
  195.0 11.8 %all-reduce.1 = f32[512]{0:T(512)S(1)} all-reduce(f32[512]{0:T(512)S(1)} %get-tuple-element.287), channel_id=1, replica_groups=mesh['grp'=4,'mem'=8] {'mem'}, use_global_device_ids=true, to_apply=%add.1 | all-reduce | flops 512 | bytes 4096
  206.8 8.6 %all_gather.15 = f32[512,64]{1,0:T(8,128)S(1)} all-gather(f32[64,64]{1,0:T(8,128)S(1)} %get-tuple-element.278), channel_id=1, replica_groups=mesh['grp'=4,'mem'=8] {'mem'}, dimensions={0}, use_global_device_ids=true | all-gather | bytes 147456 | tf_op jit(solution)/shard_map/all_gather | solution.py:127
  215.9 12.2 %while.41 = (s32[]{:T(128)}, f32[512,128]{1,0:T(8,128)}, f32[512]{0:T(512)S(1)}, f32[512]{0:T(512)S(1)}, f32[2,1024,128]{2,1,0:T(8,128)S(1)}, /*index=5*/f32[512...) while((s32[]{:T(128)}, f32[512,128]{1,0:T(8,128)}, ...), condition=%wide.region_24.25_spmd.clone, body=%wide.region_20.24_spmd.clone.sunk | while | flops 1617559040 | bytes 10293372 | solution.py:70
  215.9 2.0 fusion.76
  218.3 0.5 fusion.78
  218.8 2.7 convolution_add_fusion.5
  221.6 2.0 fusion.76
  223.9 0.5 fusion.78
  224.5 3.7 %convolution_add_fusion.5 = f32[512,128]{1,0:T(8,128)} fusion(f32[2,1024,128]{2,1,0:T(8,128)S(1)} %get-tuple-element.513, s32[]{:T(128)} %get-tuple-element.499, f32[1024,512]{0,1:T(8,128)S(1)} %get-tuple-element.433, f32[1024]{0:T(1024)S(1)} %bitcast.105, f32[1024]{0:T(1024)S(1)} %fusion.77, f32[1024]{0:T(1024)S(1)} %get-tuple-element.434, ...), kind=kOutput, calls=%fused_computation.35.clone.1 | convolution fusion | flops 807010304 | bytes 3158021 | tf_op jit(solution)/shard_map/while/body/eval_jaxpr/dot_general | solution.py:56
  228.1 13.2 %all-reduce.4 = f32[512]{0:T(512)S(1)} all-reduce(f32[512]{0:T(512)S(1)} %get-tuple-element.132), channel_id=7, replica_groups=mesh['grp'=4,'mem'=8] {'mem'}, use_global_device_ids=true, to_apply=%region_27.28.clone | all-reduce | flops 512 | bytes 4096
  241.4 17.8 %reduce-scatter.8.cloned.1.call-done = f32[64,128]{1,0:T(8,128)} async-done(((f32[512,128]{1,0:T(8,128)}), f32[64,128]{1,0:T(8,128)}) %reduce-scatter.8.cloned.1.call-update) | async-done | bytes 32784 | tf_op jit(solution)/shard_map/reduce_scatter | solution.py:118
  259.2 19.8 %all-reduce.5 = (f32[64,128]{1,0:T(8,128)S(1)}, f32[64]{0:T(128)S(1)}) all-reduce(f32[64,128]{1,0:T(8,128)} %reduce-scatter.8.cloned.1.call-done, f32[64]{0:T(128)S(1)} %dynamic-slice.7), channel_id=1, replica_groups=mesh['grp'=4,'mem'=8] {'grp'}, use_global_device_ids=true, to_apply=%region_26.27 | all-reduce | flops 8256 | bytes 66048 | tf_op jit(solution)/shard_map/psum | solution.py:121
  279.1 0.5 broadcast_divide_fusion
  279.6 0.7 fusion.39
  (75 shorter events, 3.1 us)
Async XLA Ops:
  7.2 70.4 %reduce-scatter.4.cloned.1.call-start = ((), (), s32[]{:S(2)}) async-start(), calls=%async_computation.3 | async-start | bytes 294912 | tf_op jit(solution)/shard_map/reduce_scatter | solution.py:118
  8.5 1.5 copy-start.2
  8.5 1.6 copy-start.1
  10.1 51.9 %copy-start.3 = (u32[32]{0:T(128)S(1)}, u32[32]{0:T(128)}, u32[]{:S(2)}) copy-start(u32[32]{0:T(128)} %constant.66) | copy-start | bytes 388
  18.5 0.7 copy-start
  19.2 148.6 %reduce-scatter.6.cloned.1.call-start = ((), (), s32[]{:S(2)}) async-start(), calls=%async_computation.4 | async-start | bytes 294912 | tf_op jit(solution)/shard_map/reduce_scatter | solution.py:118
  96.5 1.3 collective-permute-start
  97.8 4.3 %collective-permute-start.1 = (f32[2,64,64]{2,1,0:T(8,128)S(1)}, f32[2,64,64]{2,1,0:T(8,128)S(1)}, u32[]{:S(2)}, u32[]{:S(2)}) collective-permute-start(f32[2,64,64]{2,1,0:T(8,128)S(1)} %get-tuple-element.277), channel_id=1, source_target_pairs={{0,2},{1,3},{2,0},{3,1},{4,6},{5,7},{6,4},{7,5},{8,10},{9,11},{10,... | collective-permute-start | bytes 98312 | tf_op jit(solution)/shard_map/ppermute | solution.py:26
  102.1 21.8 %collective-permute-start.2 = (f32[4,64,64]{2,1,0:T(8,128)S(1)}, f32[4,64,64]{2,1,0:T(8,128)S(1)}, u32[]{:S(2)}, u32[]{:S(2)}) collective-permute-start(f32[4,64,64]{2,1,0:T(8,128)S(1)} %bitcast.106), channel_id=1, source_target_pairs={{0,4},{1,5},{2,6},{3,7},{4,0},{5,1},{6,2},{7,3},{8,12},{9,13},{10,... | collective-permute-start | bytes 196616 | tf_op jit(solution)/shard_map/ppermute | solution.py:26
  136.7 122.6 %reduce-scatter.8.cloned.1.call-start = ((), (), s32[]{:S(2)}) async-start(), calls=%async_computation.5 | async-start | bytes 294912 | tf_op jit(solution)/shard_map/reduce_scatter | solution.py:118
  187.8 1.3 collective-permute-start.3
  189.1 4.3 %collective-permute-start.4 = (f32[2,64,64]{2,1,0:T(8,128)S(1)}, f32[2,64,64]{2,1,0:T(8,128)S(1)}, u32[]{:S(2)}, u32[]{:S(2)}) collective-permute-start(f32[2,64,64]{2,1,0:T(8,128)S(1)} %get-tuple-element.275), channel_id=1, source_target_pairs={{0,2},{1,3},{2,0},{3,1},{4,6},{5,7},{6,4},{7,5},{8,10},{9,11},{10,... | collective-permute-start | bytes 98312 | tf_op jit(solution)/shard_map/ppermute | solution.py:26
  193.5 22.0 %collective-permute-start.5 = (f32[4,64,64]{2,1,0:T(8,128)S(1)}, f32[4,64,64]{2,1,0:T(8,128)S(1)}, u32[]{:S(2)}, u32[]{:S(2)}) collective-permute-start(f32[4,64,64]{2,1,0:T(8,128)S(1)} %bitcast.108), channel_id=1, source_target_pairs={{0,4},{1,5},{2,6},{3,7},{4,0},{5,1},{6,2},{7,3},{8,12},{9,13},{10,... | collective-permute-start | bytes 196616 | tf_op jit(solution)/shard_map/ppermute | solution.py:26
Sparse Core Ops, SparseCore 0:
  19.3 36.3 reduce-scatter.3
  136.8 30.9 reduce-scatter.5
  228.3 30.9 reduce-scatter.7
